TPU v7x, 128 devices: a whole 4x4x4 slice. The times are simulated.
128 devices in a mesh: dp: 16 (over x, y), tensor: 8 (over z, core).
Axes of the slice: x: 4, y: 4, z: 4, core: 2. Of those that a mesh axis runs over, the one named last changes fastest.
Arguments:
- hidden_rows: bfloat16 [256, 32, 8192], P('tensor', 'dp'), may hold values from -6 to 6
- norm_gain: float32 [8192], replicated, may hold values from 0.1 to 1.9
- w_query: bfloat16 [8192, 4096], P(None, 'tensor'), may hold values from -0.0625 to 0.0625
- w_key: bfloat16 [8192, 1024], P(None, 'tensor'), may hold values from -0.0625 to 0.0625
- w_value: bfloat16 [8192, 1024], P(None, 'tensor'), may hold values from -0.0625 to 0.0625
- w_out: bfloat16 [4096, 8192], P('tensor'), may hold values from -1.5 to 1.5
- cache_keys: bfloat16 [32, 2048, 1024], P('dp', None, 'tensor'), may hold values from -6 to 6
- cache_values: bfloat16 [32, 2048, 1024], P('dp', None, 'tensor'), may hold values from -6 to 6
- slot_of_request: int32 [32], replicated, may hold values from 0 to 31, as said below
- span_length: int32 [32], replicated, may hold values from 1 to 256, as said below
- prefix_length: int32 [32], replicated, may hold values from 1 to 2048, as said below
Outputs:
- attention_out: bfloat16 [256, 32, 8192], P('tensor', 'dp')
Inputs may be any that keep to these rules, and one draw needn't show every extreme that they name: `slot_of_request`: a permutation of the slots 0 to 31; slot i lies on dp index i // 2, request r starts on dp index r // 2; there are 2 distinct numbers m, one of them 1, the same for every dp index, such that the 2 requests of dp index i have their slots on the dp indices i XOR m, one on each. `span_length`: some request uses all 256 new positions. `prefix_length`: some request has all 2048 cached positions.
All inputs are finite; a program needn't handle non-finite values.
Results may differ from a plain program's by a relative error of at most 0.019.
Values may be sent and summed in bfloat16 or wider, within the bound.
A program may use at most 128 MiB of HBM per device.

v0:
```python
import jax
import jax.numpy as jnp
from jax import lax
from jax.sharding import PartitionSpec as P

HD = 128
rope_base = 500000.0
norm_eps = 1e-05
masked = -1e30


def rotate(values, position):
    head_width = values.shape[-1]
    half_width = head_width // 2
    frequency = rope_base ** (-(jnp.arange(half_width, dtype=jnp.float32) * 2.0 / head_width))
    angles = position[..., None, None] * frequency
    cosine = jnp.cos(angles)
    sine_part = jnp.sin(angles)
    front_half = values[..., :half_width]
    back_half = values[..., half_width:]
    return jnp.concatenate(
        [front_half * cosine - back_half * sine_part, back_half * cosine + front_half * sine_part],
        axis=-1,
    )


def normalize(hidden_rows, norm_gain):
    floats = hidden_rows.astype(jnp.float32)
    return (
        floats * lax.rsqrt(jnp.mean(floats * floats, axis=-1, keepdims=True) + norm_eps) * norm_gain
    ).astype(jnp.bfloat16)


def project_group(normed, prefix_here, w_query, w_key, w_value):
    piece_rows = lax.all_gather(normed, "tensor", axis=0, tiled=True)
    row_count = piece_rows.shape[0]
    request_count = piece_rows.shape[1]
    positions = (prefix_here[None, :] + jnp.arange(row_count, dtype=jnp.int32)[:, None]).astype(
        jnp.float32
    )
    queries = jnp.einsum("nsd,df->nsf", piece_rows, w_query, preferred_element_type=jnp.float32)
    queries = rotate(queries.reshape(row_count, request_count, -1, HD), positions)
    keys_new = jnp.einsum("nsd,df->nsf", piece_rows, w_key, preferred_element_type=jnp.float32)
    keys_new = rotate(keys_new.reshape(row_count, request_count, -1, HD), positions)
    values_new = jnp.einsum("nsd,df->nsf", piece_rows, w_value, preferred_element_type=jnp.float32)
    return jnp.concatenate(
        [
            queries.reshape(row_count, request_count, -1).astype(jnp.bfloat16),
            keys_new.reshape(row_count, request_count, -1).astype(jnp.bfloat16),
            values_new.astype(jnp.bfloat16),
        ],
        axis=-1,
    )


def attend_slots(packed, cache_keys, cache_values, slot_prefix, slot_length, q_width, kv_width):
    span_rows = packed.shape[0]
    slot_count = packed.shape[1]
    kv_heads = kv_width // HD
    groups = q_width // kv_width
    prefix = cache_keys.shape[1]
    score_scale = HD ** (-0.5)
    queries = packed[..., :q_width].reshape(span_rows, slot_count, kv_heads, groups, HD)
    keys_new = packed[..., q_width : q_width + kv_width].reshape(
        span_rows, slot_count, kv_heads, HD
    )
    values_new = packed[..., q_width + kv_width :].reshape(span_rows, slot_count, kv_heads, HD)
    keys_old = cache_keys.reshape(slot_count, prefix, kv_heads, HD)
    values_old = cache_values.reshape(slot_count, prefix, kv_heads, HD)
    score_old = (
        jnp.einsum("csgmd,spgd->sgmcp", queries, keys_old, preferred_element_type=jnp.float32)
        * score_scale
    )
    score_new = (
        jnp.einsum("csgmd,jsgd->sgmcj", queries, keys_new, preferred_element_type=jnp.float32)
        * score_scale
    )
    keep_old = jnp.arange(prefix, dtype=jnp.int32)[None, :] < slot_prefix[:, None]
    row_index = jnp.arange(span_rows, dtype=jnp.int32)
    keep_new = (row_index[None, None, :] < slot_length[:, None, None]) & (
        row_index[None, None, :] <= row_index[None, :, None]
    )
    score_old = jnp.where(keep_old[:, None, None, None, :], score_old, masked)
    score_new = jnp.where(keep_new[:, None, None, :, :], score_new, masked)
    exp_old = jnp.exp(score_old)
    exp_new = jnp.exp(score_new)
    denominator = jnp.sum(exp_old, axis=-1, keepdims=True) + jnp.sum(
        exp_new, axis=-1, keepdims=True
    )
    weight_old = (exp_old / denominator).astype(jnp.bfloat16)
    weight_new = (exp_new / denominator).astype(jnp.bfloat16)
    mixed = jnp.einsum(
        "sgmcp,spgd->csgmd", weight_old, values_old, preferred_element_type=jnp.float32
    )
    mixed = mixed + jnp.einsum(
        "sgmcj,jsgd->csgmd", weight_new, values_new, preferred_element_type=jnp.float32
    )
    return mixed.astype(jnp.bfloat16).reshape(span_rows, slot_count, q_width)


def local(
    hidden_rows,
    norm_gain,
    w_query,
    w_key,
    w_value,
    w_out,
    cache_keys,
    cache_values,
    slot_of_request,
    span_length,
    prefix_length,
):
    data_size = lax.axis_size("dp")
    data_index = lax.axis_index("dp")
    per_device = hidden_rows.shape[1]
    q_width = w_query.shape[1]
    kv_width = w_key.shape[1]
    all_requests = slot_of_request.shape[0]
    request_ids = jnp.arange(all_requests, dtype=jnp.int32)
    devices = jnp.arange(data_size, dtype=jnp.int32)
    first_request = data_index * per_device
    my_slots = lax.dynamic_slice_in_dim(slot_of_request, first_request, per_device)
    send_table = (devices[:, None] == my_slots[None, :] // per_device).astype(jnp.bfloat16)
    slot_match = (
        slot_of_request[None, :]
        == (first_request + jnp.arange(per_device, dtype=jnp.int32))[:, None]
    )
    source_match = request_ids[None, :] // per_device == devices[:, None]
    recv_table = jnp.any(slot_match[:, None, :] & source_match[None, :, :], axis=-1).astype(
        jnp.bfloat16
    )
    slot_prefix = jnp.sum(jnp.where(slot_match, prefix_length[None, :], 0), axis=1)
    slot_length = jnp.sum(jnp.where(slot_match, span_length[None, :], 0), axis=1)
    normed = normalize(hidden_rows, norm_gain)
    outgoing = jnp.einsum(
        "js,csf->jcf", send_table, normed, preferred_element_type=jnp.float32
    ).astype(jnp.bfloat16)
    incoming = lax.all_to_all(outgoing, "dp", split_axis=0, concat_axis=0, tiled=True)
    slot_rows = jnp.einsum(
        "sj,jcf->csf", recv_table, incoming, preferred_element_type=jnp.float32
    ).astype(jnp.bfloat16)
    packed = project_group(slot_rows, slot_prefix, w_query, w_key, w_value)
    mixed = attend_slots(
        packed, cache_keys, cache_values, slot_prefix, slot_length, q_width, kv_width
    )
    outgoing_back = jnp.einsum(
        "sj,csf->jcf", recv_table, mixed, preferred_element_type=jnp.float32
    ).astype(jnp.bfloat16)
    returned = lax.all_to_all(outgoing_back, "dp", split_axis=0, concat_axis=0, tiled=True)
    request_heads = jnp.einsum(
        "js,jcf->csf", send_table, returned, preferred_element_type=jnp.float32
    ).astype(jnp.bfloat16)
    span_rows = request_heads.shape[0]
    flat_heads = request_heads.reshape(span_rows * per_device, q_width)
    summed = lax.psum_scatter(
        jnp.dot(flat_heads, w_out, preferred_element_type=jnp.float32).astype(jnp.bfloat16),
        "tensor",
        scatter_dimension=0,
        tiled=True,
    ).astype(jnp.float32)
    return summed.reshape(hidden_rows.shape[0], per_device, -1).astype(jnp.bfloat16)


def solution(mesh):
    placed = (
        P("tensor", "dp", None),
        P(),
        P(None, "tensor"),
        P(None, "tensor"),
        P(None, "tensor"),
        P("tensor", None),
        P("dp", None, "tensor"),
        P("dp", None, "tensor"),
        P(),
        P(),
        P(),
    )
    return jax.shard_map(
        local, mesh=mesh, in_specs=placed, out_specs=P("tensor", "dp", None), check_vma=False
    )
```

profile of v0, /device:TPU:1, one launch (start us, length us, event | category | flops | bytes accessed | tf_op | source)
XLA Modules:
  0.0 441.6 jit_solution(15629852325169047121)
XLA Ops:
  6.5 2.6 fusion.16
  9.1 0.7 and_select_fusion
  9.8 7.6 %convolution_convert_fusion.1 = bf16[16,32,8192]{2,0,1:T(8,128)(2,1)} fusion(bf16[32,2,8192]{2,1,0:T(2,128)(2,1)} %param.11, f32[8192]{0:T(1024)} %param.12, f32[32,2]{1,0:T(8,128)S(1)} %add_rsqrt_fusion, s32[2]{0:T(128)S(1)} %and_select_fusion), kind=kOutput, calls=%fused_computation.6 | convolution fusion | flops 23068704 | bytes 9470216 | tf_op jit(solution)/shard_map/js,csf->jcf/dot_general | solution.py:136
  17.5 11.2 %copy.63 = bf16[16,32,8192]{2,1,0:T(8,128)(2,1)} copy(bf16[16,32,8192]{2,0,1:T(8,128)(2,1)} %convolution_convert_fusion.1) | data formatting | bytes 16777216 | tf_op jit(solution)/shard_map/convert_element_type | solution.py:138
  28.7 7.8 %all-to-all-start = ((bf16[16,32,8192]{2,1,0:T(8,128)(2,1)}), bf16[16,32,8192]{2,1,0:T(8,128)(2,1)}, u32[]{:S(2)}, u32[]{:S(2)}) async-start(bf16[16,32,8192]{2,1,0:T(8,128)(2,1)} %copy.63), calls=%async_computation | async-start | bytes 16777216 | tf_op jit(solution)/shard_map/all_to_all | solution.py:139
  36.4 0.2 all-gather.2.cloned.1.call-start
  36.7 0.2 select_reduce_fusion
  37.0 145.5 %all-to-all-done = bf16[16,32,8192]{2,1,0:T(8,128)(2,1)} async-done(((bf16[16,32,8192]{2,1,0:T(8,128)(2,1)}), bf16[16,32,8192]{2,1,0:T(8,128)(2,1)}, u32[]{:S(2)}, u32[]{:S(2)}) %all-to-all-start) | async-done | bytes 8388640 | tf_op jit(solution)/shard_map/all_to_all | solution.py:139
  182.5 9.4 %fusion.3 = bf16[32,2,8192]{2,1,0:T(2,128)(2,1)} fusion(bf16[16,32,8192]{2,1,0:T(8,128)(2,1)} %all-to-all-done, pred[2,16]{1,0:T(4,128)(4,1)S(1)} %and_reduce_fusion), kind=kOutput, calls=%fused_computation.8 | convolution fusion | flops 17301504 | bytes 9437216 | tf_op jit(solution)/shard_map/sj,jcf->csf/dot_general | solution.py:140
  191.9 0.3 reduce-scatter.2.cloned.1.call-start
  192.4 0.1 broadcast_and_fusion
  192.5 1.7 multiply_cosine_fusion
  194.4 53.7 %all-gather.2.cloned.1.call-done = bf16[256,2,8192]{2,1,0:T(2,128)(2,1)} async-done(((bf16[32,2,8192]{2,1,0:T(2,128)(2,1)}), bf16[256,2,8192]{2,1,0:T(2,128)(2,1)}) %all-gather.2.cloned.1.call-update) | async-done | bytes 8388624 | tf_op jit(solution)/shard_map/all_gather | solution.py:35
  248.0 8.9 %fusion.38 = f32[256,2,1,128]{0,3,1,2:T(8,128)S(1)} fusion(bf16[8192,128]{1,0:T(8,128)(2,1)} %param.14, bf16[256,2,8192]{2,1,0:T(2,128)(2,1)} %all-gather.2.cloned.1.call-done), kind=kOutput, calls=%fused_computation.38 | convolution fusion | flops 1073741824 | bytes 10747904 | tf_op jit(solution)/shard_map/nsd,df->nsf/dot_general | solution.py:43
  256.9 1.2 fusion.78
  258.1 13.0 %fusion.6 = f32[256,2,512]{2,0,1:T(8,128)} fusion(bf16[8192,512]{1,0:T(8,128)(2,1)} %param.13, bf16[256,2,8192]{2,1,0:T(2,128)(2,1)S(1)} %copy-done.7), kind=kOutput, calls=%fused_computation.11 | convolution fusion | flops 4294967296 | bytes 17825792 | tf_op jit(solution)/shard_map/nsd,df->nsf/dot_general | solution.py:41
  271.1 1.6 reshape.282
  272.7 0.6 fusion.91
  273.3 1.2 subtract_convert_fusion
  274.5 9.1 %fusion.2 = (f32[2,4,256]{2,1,0:T(4,128)S(1)}, f32[2,256,4,2048]{3,1,2,0:T(8,128)}) fusion(pred[2,2048]{1,0:T(4,128)(4,1)S(1)} %iota_compare_fusion.1, bf16[2,2048,128]{2,1,0:T(8,128)(2,1)} %param.17, bf16[256,2,4,64]{3,0,2,1:T(8,128)(2,1)S(1)} %get-tuple-element.9, bf16[256,2,4,64]{3,0,2,1:T(8,128)(2,1)S(1)} %get-tuple-element.8), kind=kOutput, calls=%fused_computation.4 | convolution fusion | flops 1087371264 | bytes 18362368 | tf_op jit(solution)/shard_map/csgmd,spgd->sgmcp/dot_general | solution.py:71
  283.6 2.1 fusion.22
  285.8 14.5 %fusion.57 = f32[2,128,4,256]{3,1,2,0:T(8,128)} fusion(f32[2,256,256,4]{2,1,3,0:T(8,128)} %get-tuple-element.19, f32[2,4,256]{2,1,0:T(4,128)S(1)} %add.80, pred[2,256,256]{1,2,0:T(8,128)(4,1)S(1)} %broadcast_and_fusion, bf16[8192,128]{1,0:T(8,128)(2,1)S(1)} %copy-done, bf16[256,2,8192]{2,1,0:T(2,128)(2,1)} %all-gather.2.cloned.1.call-done), kind=kOutput, calls=%fused_computation.44 | convolution fusion | flops 1210122240 | bytes 13770752 | tf_op jit(solution)/shard_map/sgmcj,jsgd->csgmd/dot_general | solution.py:95
  300.3 8.0 %fusion.32 = bf16[2,128,4,256]{3,1,2,0:T(8,128)(2,1)S(1)} fusion(f32[2,128,4,256]{3,1,2,0:T(8,128)} %fusion.57, f32[2,4,256]{2,1,0:T(4,128)S(1)} %add.80, f32[2,256,4,2048]{3,1,2,0:T(8,128)} %get-tuple-element.17, pred[2,2048]{1,0:T(4,128)(4,1)S(1)} %iota_compare_fusion.1, bf16[2,2048,128]{2,1,0:T(8,128)(2,1)S(1)} %copy-done.8), kind=kOutput, calls=%fused_computation.36 | convolution fusion | flops 1091043328 | bytes 19410944 | tf_op jit(solution)/shard_map/sgmcp,spgd->csgmd/dot_general | solution.py:92
  308.3 0.5 copy.75
  308.8 1.6 convolution_convert_fusion.3
  310.5 2.4 copy.76
  312.9 56.0 %all_to_all.10 = bf16[16,256,512]{2,1,0:T(8,128)(2,1)S(1)} all-to-all(bf16[16,256,512]{2,1,0:T(8,128)(2,1)S(1)} %copy.76), channel_id=1, replica_groups=mesh['dp'=16,'tensor'=8] {'dp'}, dimensions={0} | all-to-all | bytes 8388608 | tf_op jit(solution)/shard_map/all_to_all | solution.py:150
  368.8 2.5 fusion.35
  371.4 0.2 reshape.287
  371.6 10.2 %convolution_convert_fusion = bf16[512,8192]{1,0:T(8,128)(2,1)} fusion(bf16[512,512]{1,0:T(8,128)(2,1)S(1)} %reshape.287, bf16[512,8192]{1,0:T(8,128)(2,1)} %param.16), kind=kOutput, calls=%fused_computation.5 | convolution fusion | flops 4299161600 | bytes 17301504 | tf_op jit(solution)/shard_map/dot_general | solution.py:157
  381.8 50.2 %reduce-scatter.2.cloned.1.call-done = bf16[64,8192]{1,0:T(8,128)(2,1)} async-done(((bf16[512,8192]{1,0:T(8,128)(2,1)}), bf16[64,8192]{1,0:T(8,128)(2,1)}) %reduce-scatter.2.cloned.1.call-update) | async-done | bytes 1048592 | tf_op jit(solution)/shard_map/reduce_scatter | solution.py:156
  432.1 2.5 convert_element_type.82
  (31 shorter events, 0.5 us)
Async XLA Ops:
  6.5 279.2 %copy-start = (bf16[8192,128]{1,0:T(8,128)(2,1)S(1)}, bf16[8192,128]{1,0:T(8,128)(2,1)}, u32[]{:S(2)}) copy-start(bf16[8192,128]{1,0:T(8,128)(2,1)} %param.15) | copy-start | bytes 6291460
  28.6 8.0 %copy-start.4 = (s32[32]{0:T(128)S(1)}, s32[32]{0:T(128)}, u32[]{:S(2)}) copy-start(s32[32]{0:T(128)} %param.19) | copy-start | bytes 388
  28.7 8.0 %copy-start.5 = (s32[32]{0:T(128)S(1)}, s32[32]{0:T(128)}, u32[]{:S(2)}) copy-start(s32[32]{0:T(128)} %param.20) | copy-start | bytes 388
  28.7 8.1 %copy-start.6 = (s32[32]{0:T(128)S(1)}, s32[32]{0:T(128)}, u32[]{:S(2)}) copy-start(s32[32]{0:T(128)} %param.21) | copy-start | bytes 388
  28.7 153.8 %all-to-all-start = ((bf16[16,32,8192]{2,1,0:T(8,128)(2,1)}), bf16[16,32,8192]{2,1,0:T(8,128)(2,1)}, u32[]{:S(2)}, u32[]{:S(2)}) async-start(bf16[16,32,8192]{2,1,0:T(8,128)(2,1)} %copy.63), calls=%async_computation | async-start | bytes 16777216 | tf_op jit(solution)/shard_map/all_to_all | solution.py:139
  36.4 211.6 %all-gather.2.cloned.1.call-start = ((), (), s32[]{:S(2)}) async-start(), calls=%async_computation.3 | async-start | bytes 9437184 | tf_op jit(solution)/shard_map/all_gather | solution.py:35
  191.9 240.1 %reduce-scatter.2.cloned.1.call-start = ((), (), s32[]{:S(2)}) async-start(), calls=%async_computation.4 | async-start | bytes 9437184 | tf_op jit(solution)/shard_map/reduce_scatter | solution.py:156
  248.0 10.1 %copy-start.7 = (bf16[256,2,8192]{2,1,0:T(2,128)(2,1)S(1)}, bf16[256,2,8192]{2,1,0:T(2,128)(2,1)}, u32[]{:S(2)}) copy-start(bf16[256,2,8192]{2,1,0:T(2,128)(2,1)} %all-gather.2.cloned.1.call-done) | copy-start | bytes 25165828
  274.5 9.1 %copy-start.2 = (bf16[256,2,64]{0,2,1:T(8,128)(2,1)S(1)}, bf16[256,2,64]{0,2,1:T(8,128)(2,1)}, u32[]{:S(2)}) copy-start(bf16[256,2,64]{0,2,1:T(8,128)(2,1)} %get-tuple-element.12) | copy-start | bytes 196612
  274.5 9.1 %copy-start.3 = (bf16[256,2,64]{0,2,1:T(8,128)(2,1)S(1)}, bf16[256,2,64]{0,2,1:T(8,128)(2,1)}, u32[]{:S(2)}) copy-start(bf16[256,2,64]{0,2,1:T(8,128)(2,1)} %get-tuple-element.13) | copy-start | bytes 196612
  285.8 14.5 %copy-start.8 = (bf16[2,2048,128]{2,1,0:T(8,128)(2,1)S(1)}, bf16[2,2048,128]{2,1,0:T(8,128)(2,1)}, u32[]{:S(2)}) copy-start(bf16[2,2048,128]{2,1,0:T(8,128)(2,1)} %param.18) | copy-start | bytes 3145732
  371.6 63.0 %copy-start.1 = (bf16[8192,128]{1,0:T(8,128)(2,1)S(1)}, bf16[8192,128]{1,0:T(8,128)(2,1)}, u32[]{:S(2)}) copy-start(bf16[8192,128]{1,0:T(8,128)(2,1)} %param.15) | copy-start | bytes 6291460
Sparse Core Ops, SparseCore 0:
  192.1 55.9 all-gather.1
  382.0 50.0 reduce-scatter.1
where the time goes:
time: 448 us; the launch traced here: 442 us
  waiting for transfers between devices  249 us (56%)
  matrix products  87 us (19%)
  blocking collectives  56 us (12%)
  local copies, waits for them, and re-layouts  19 us (4%)
  between operations  13.8 us (3%)
  starting transfers between devices  8.23 us (2%)
  other arithmetic  8.21 us (2%)
    all_to_all x1, waiting for transfers between devices, local(): lax.all_to_all(outgoing, 'dp', split_axis=0, concat_axis=0, tiled=True)  145 us
    all_to_all x1, blocking collectives, local(): lax.all_to_all(outgoing_back, 'dp', split_axis=0, concat_axis=0, tiled=True)  56 us
    all_gather x1, waiting for transfers between devices, project_group(): piece_rows = lax.all_gather(normed, 'tensor', axis=0, tiled=True)  53.7 us
    reduce_scatter x1, waiting for transfers between devices, local(): lax.psum_scatter(jnp.dot(flat_heads, w_out, preferred_element_type=jnp.fl...  50.2 us
    dot_general x1, matrix products, attend_slots(): jnp.einsum('sgmcj,jsgd->csgmd', weight_new, values_new, preferred_element...  14.5 us
    dot_general x1, matrix products, project_group(): jnp.einsum('nsd,df->nsf', piece_rows, w_query, preferred_element_type=jnp...  13 us
    convert_element_type x1, local copies, waits for them, and re-layouts, local(): outgoing = jnp.einsum('js,csf->jcf', send_table, normed, preferred_elemen...  11.2 us
    dot_general x1, matrix products, local(): jnp.dot(flat_heads, w_out, preferred_element_type=jnp.float32)  10.2 us
  transfers between devices with their start and end apart: 3, of which 3 were waited for; matrix products, arithmetic and copies ran while one was open for 1% of the time, Pallas kernels for 0%

commit v1 on v0

--- a/solution.py
+++ b/solution.py
@@ -32,7 +32,9 @@
 
 
 def project_group(normed, prefix_here, w_query, w_key, w_value):
-    piece_rows = lax.all_gather(normed, "tensor", axis=0, tiled=True)
+    piece_rows = jnp.concatenate(
+        lax.all_to_all(jnp.stack([normed] * lax.axis_size("tensor")), "tensor", 0, 0), axis=0
+    )
     row_count = piece_rows.shape[0]
     request_count = piece_rows.shape[1]
     positions = (prefix_here[None, :] + jnp.arange(row_count, dtype=jnp.int32)[:, None]).astype(

time: 448 us -> 488 us (1.089)
  waiting for transfers between devices: 249 us -> 277 us
  local copies, waits for them, and re-layouts: 19 us -> 40.7 us
  matrix products: 87 us -> 70.2 us
  starting transfers between devices: 8.23 us -> 16.1 us
    all_to_all x0 -> x1, waiting for transfers between devices: none -> 81.4 us  [project_group(): lax.all_to_all(jnp.stack([normed] * lax.axis_size('tensor')), 'tensor', 0...]
    all_gather x1 -> x0, waiting for transfers between devices: 53.7 us -> none  [project_group(): piece_rows = lax.all_gather(normed, 'tensor', axis=0, tiled=True)]
    dot_general x0 -> x1, local copies, waits for them, and re-layouts: none -> 11.3 us  [project_group(): jnp.einsum('nsd,df->nsf', piece_rows, w_query, preferred_element_type=jnp...]
    all_to_all x0 -> x1, local copies, waits for them, and re-layouts: none -> 7.74 us  [project_group(): lax.all_to_all(jnp.stack([normed] * lax.axis_size('tensor')), 'tensor', 0...]
    all_to_all x0 -> x1, starting transfers between devices: none -> 7.64 us  [project_group(): lax.all_to_all(jnp.stack([normed] * lax.axis_size('tensor')), 'tensor', 0...]
    dot_general x1, matrix products: 14.5 us -> 7.89 us  [attend_slots(): jnp.einsum('sgmcj,jsgd->csgmd', weight_new, values_new, preferred_element...]
    dot_general x1, matrix products: 13 us -> 7.04 us  [project_group(): jnp.einsum('nsd,df->nsf', piece_rows, w_query, preferred_element_type=jnp...]
  transfers between devices with their start and end apart: 3 -> 3, of which waited for: 3 -> 3; matrix products, arithmetic and copies ran while one was open for 1% -> 3% of each run, Pallas kernels for 0% -> 0%
where the time goes in v1:
time: 488 us; the launch traced here: 481 us
  waiting for transfers between devices  277 us (57%)
  matrix products  70.2 us (14%)
  blocking collectives  58.1 us (12%)
  local copies, waits for them, and re-layouts  40.7 us (8%)
  starting transfers between devices  16.1 us (3%)
  between operations  13.8 us (3%)
  other arithmetic  5.29 us (1%)
    all_to_all x1, waiting for transfers between devices, local(): lax.all_to_all(outgoing, 'dp', split_axis=0, concat_axis=0, tiled=True)  146 us
    all_to_all x1, waiting for transfers between devices, project_group(): lax.all_to_all(jnp.stack([normed] * lax.axis_size('tensor')), 'tensor', 0...  81.4 us
    all_to_all x1, blocking collectives, local(): lax.all_to_all(outgoing_back, 'dp', split_axis=0, concat_axis=0, tiled=True)  58.1 us
    reduce_scatter x1, waiting for transfers between devices, local(): lax.psum_scatter(jnp.dot(flat_heads, w_out, preferred_element_type=jnp.fl...  49.8 us
    dot_general x1, local copies, waits for them, and re-layouts, project_group(): jnp.einsum('nsd,df->nsf', piece_rows, w_query, preferred_element_type=jnp...  11.3 us
    convert_element_type x1, local copies, waits for them, and re-layouts, local(): outgoing = jnp.einsum('js,csf->jcf', send_table, normed, preferred_elemen...  11.2 us
    dot_general x1, matrix products, local(): jnp.dot(flat_heads, w_out, preferred_element_type=jnp.float32)  10.2 us
  transfers between devices with their start and end apart: 3, of which 3 were waited for; matrix products, arithmetic and copies ran while one was open for 3% of the time, Pallas kernels for 0%

profile of v1, /device:TPU:1, one launch (start us, length us, event | category | flops | bytes accessed | tf_op | source)
XLA Modules:
  0.0 481.1 jit_solution(15073457416843971495)
XLA Ops:
  6.5 2.6 fusion.9
  9.1 0.7 and_select_fusion
  9.8 7.7 %convolution_convert_fusion.1 = bf16[16,32,8192]{2,0,1:T(8,128)(2,1)} fusion(bf16[32,2,8192]{2,1,0:T(2,128)(2,1)} %param.11, f32[8192]{0:T(1024)} %param.12, f32[32,2]{1,0:T(8,128)S(1)} %add_rsqrt_fusion, s32[2]{0:T(128)S(1)} %and_select_fusion), kind=kOutput, calls=%fused_computation.6 | convolution fusion | flops 23068704 | bytes 9470216 | tf_op jit(solution)/shard_map/js,csf->jcf/dot_general | solution.py:138
  17.5 11.2 %copy.64 = bf16[16,32,8192]{2,1,0:T(8,128)(2,1)} copy(bf16[16,32,8192]{2,0,1:T(8,128)(2,1)} %convolution_convert_fusion.1) | data formatting | bytes 16777216 | tf_op jit(solution)/shard_map/convert_element_type | solution.py:140
  28.7 8.2 %all-to-all-start = ((bf16[16,32,8192]{2,1,0:T(8,128)(2,1)}), bf16[16,32,8192]{2,1,0:T(8,128)(2,1)}, u32[]{:S(2)}, u32[]{:S(2)}) async-start(bf16[16,32,8192]{2,1,0:T(8,128)(2,1)} %copy.64), calls=%async_computation | async-start | bytes 16777216 | tf_op jit(solution)/shard_map/all_to_all | solution.py:141
  37.1 0.2 select_reduce_fusion
  37.4 145.7 %all-to-all-done = bf16[16,32,8192]{2,1,0:T(8,128)(2,1)} async-done(((bf16[16,32,8192]{2,1,0:T(8,128)(2,1)}), bf16[16,32,8192]{2,1,0:T(8,128)(2,1)}, u32[]{:S(2)}, u32[]{:S(2)}) %all-to-all-start) | async-done | bytes 8388640 | tf_op jit(solution)/shard_map/all_to_all | solution.py:141
  183.1 8.5 %fusion.3 = bf16[32,2,8192]{2,1,0:T(2,128)(2,1)S(1)} fusion(bf16[16,32,8192]{2,1,0:T(8,128)(2,1)} %all-to-all-done, pred[2,16]{1,0:T(4,128)(4,1)S(1)} %and_reduce_fusion), kind=kOutput, calls=%fused_computation.8 | convolution fusion | flops 17301504 | bytes 9437216 | tf_op jit(solution)/shard_map/sj,jcf->csf/dot_general | solution.py:142
  191.5 0.6 copy.66
  192.1 4.2 stack.2
  196.4 7.6 %all-to-all-start.1 = ((bf16[8,32,2,8192]{3,1,2,0:T(8,128)(2,1)}), bf16[8,32,2,8192]{3,1,2,0:T(8,128)(2,1)}, u32[]{:S(2)}, u32[]{:S(2)}) async-start(bf16[8,32,2,8192]{3,1,2,0:T(8,128)(2,1)} %stack.2), calls=%async_computation.1 | async-start | bytes 16777216 | tf_op jit(solution)/shard_map/all_to_all | solution.py:36
  204.2 11.3 %copy.88 = bf16[512,8192]{1,0:T(8,128)(2,1)} copy(bf16[512,8192]{0,1:T(8,128)(2,1)} %bitcast.150) | data formatting | bytes 16777216 | tf_op jit(solution)/shard_map/nsd,df->nsf/dot_general | solution.py:43
  215.8 0.5 multiply_cosine_fusion.1
  216.4 81.4 %all-to-all-done.1 = bf16[8,32,2,8192]{3,1,2,0:T(8,128)(2,1)} async-done(((bf16[8,32,2,8192]{3,1,2,0:T(8,128)(2,1)}), bf16[8,32,2,8192]{3,1,2,0:T(8,128)(2,1)}, u32[]{:S(2)}, u32[]{:S(2)}) %all-to-all-start.1) | async-done | bytes 8388640 | tf_op jit(solution)/shard_map/all_to_all | solution.py:36
  297.8 7.7 %copy.67 = bf16[8,32,2,8192]{3,1,0,2:T(8,128)(2,1)} copy(bf16[8,32,2,8192]{3,1,2,0:T(8,128)(2,1)} %all-to-all-done.1) | data formatting | bytes 16777216 | tf_op jit(solution)/shard_map/all_to_all | solution.py:36
  305.6 6.5 %fusion.33 = f32[256,2,1,128]{0,3,1,2:T(8,128)S(1)} fusion(bf16[256,2,8192]{2,0,1:T(8,128)(2,1)} %bitcast.147, bf16[8192,128]{1,0:T(8,128)(2,1)S(1)} %copy-done.3), kind=kOutput, calls=%fused_computation.33 | convolution fusion | flops 1073741824 | bytes 10747904 | tf_op jit(solution)/shard_map/nsd,df->nsf/dot_general | solution.py:45
  312.0 0.6 fusion.65
  312.6 7.0 %fusion.78 = f32[256,2,4,128]{0,3,2,1:T(8,128)S(1)} fusion(bf16[256,2,8192,1]{2,0,3,1:T(8,128)(2,1)S(1)} %bitcast.149, bf16[4,128,8192,1]{2,1,0,3:T(8,128)(2,1)} %bitcast.151), kind=kOutput, calls=%fused_computation.99 | convolution fusion | flops 4294967296 | bytes 17825792 | tf_op jit(solution)/shard_map/nsd,df->nsf/dot_general | solution.py:43
  319.7 0.2 subtract_convert_fusion
  319.9 7.7 %fusion.2 = (f32[2,4,256]{2,1,0:T(4,128)S(1)}, f32[2,256,4,2048]{3,1,2,0:T(8,128)}) fusion(pred[2,2048]{1,0:T(4,128)(4,1)S(1)} %iota_compare_fusion.1, bf16[2,2048,128]{2,1,0:T(8,128)(2,1)S(1)} %copy-done.7, bf16[256,2,4,64]{0,3,2,1:T(8,128)(2,1)S(1)} %get-tuple-element.9, bf16[256,2,4,64]{0,3,2,1:T(8,128)(2,1)S(1)} %get-tuple-element.8), kind=kOutput, calls=%fused_computation.4 | convolution fusion | flops 1087371264 | bytes 18362368 | tf_op jit(solution)/shard_map/csgmd,spgd->sgmcp/dot_general | solution.py:73
  327.6 2.0 fusion.17
  329.6 7.9 %fusion.46 = f32[2,128,4,256]{3,1,2,0:T(8,128)} fusion(f32[2,256,256,4]{2,1,3,0:T(8,128)} %get-tuple-element.17, f32[2,4,256]{2,1,0:T(4,128)S(1)} %add.80, pred[2,256,256]{1,2,0:T(8,128)(4,1)S(1)} %broadcast_and_fusion, bf16[256,2,8192]{2,0,1:T(8,128)(2,1)} %bitcast.148, bf16[8192,128]{1,0:T(8,128)(2,1)S(1)} %copy-done), kind=kOutput, calls=%fused_computation.39 | convolution fusion | flops 1210122240 | bytes 13770752 | tf_op jit(solution)/shard_map/sgmcj,jsgd->csgmd/dot_general | solution.py:97
  337.5 8.6 %fusion.27 = bf16[2,128,4,256]{3,1,2,0:T(8,128)(2,1)S(1)} fusion(f32[2,128,4,256]{3,1,2,0:T(8,128)} %fusion.46, f32[2,4,256]{2,1,0:T(4,128)S(1)} %add.80, f32[2,256,4,2048]{3,1,2,0:T(8,128)} %get-tuple-element.15, pred[2,2048]{1,0:T(4,128)(4,1)S(1)} %iota_compare_fusion.1, bf16[2,2048,128]{2,1,0:T(8,128)(2,1)} %param.18), kind=kOutput, calls=%fused_computation.31 | convolution fusion | flops 1091043328 | bytes 19410944 | tf_op jit(solution)/shard_map/sgmcp,spgd->csgmd/dot_general | solution.py:94
  346.0 0.5 copy.76
  346.6 1.6 convolution_convert_fusion.3
  348.2 2.4 copy.77
  350.6 58.1 %all_to_all.15 = bf16[16,256,512]{2,1,0:T(8,128)(2,1)S(1)} all-to-all(bf16[16,256,512]{2,1,0:T(8,128)(2,1)S(1)} %copy.77), channel_id=1, replica_groups=mesh['dp'=16,'tensor'=8] {'dp'}, dimensions={0} | all-to-all | bytes 8388608 | tf_op jit(solution)/shard_map/all_to_all | solution.py:152
  408.7 2.5 fusion.30
  411.3 0.2 reshape.291
  411.5 10.2 %convolution_convert_fusion = bf16[512,8192]{1,0:T(8,128)(2,1)} fusion(bf16[512,512]{1,0:T(8,128)(2,1)S(1)} %reshape.291, bf16[512,8192]{1,0:T(8,128)(2,1)} %param.16), kind=kOutput, calls=%fused_computation.5 | convolution fusion | flops 4299161600 | bytes 17301504 | tf_op jit(solution)/shard_map/dot_general | solution.py:159
  421.7 49.8 %reduce-scatter.2.cloned.1.call-done = bf16[64,8192]{1,0:T(8,128)(2,1)} async-done(((bf16[512,8192]{1,0:T(8,128)(2,1)}), bf16[64,8192]{1,0:T(8,128)(2,1)}) %reduce-scatter.2.cloned.1.call-update) | async-done | bytes 1048592 | tf_op jit(solution)/shard_map/reduce_scatter | solution.py:158
  471.5 2.5 convert_element_type.82
  (30 shorter events, 0.8 us)
Async XLA Ops:
  6.5 323.0 %copy-start = (bf16[8192,128]{1,0:T(8,128)(2,1)S(1)}, bf16[8192,128]{1,0:T(8,128)(2,1)}, u32[]{:S(2)}) copy-start(bf16[8192,128]{1,0:T(8,128)(2,1)} %param.15) | copy-start | bytes 6291460
  28.7 8.3 %copy-start.4 = (s32[32]{0:T(128)S(1)}, s32[32]{0:T(128)}, u32[]{:S(2)}) copy-start(s32[32]{0:T(128)} %param.20) | copy-start | bytes 388
  28.7 8.3 %copy-start.5 = (s32[32]{0:T(128)S(1)}, s32[32]{0:T(128)}, u32[]{:S(2)}) copy-start(s32[32]{0:T(128)} %param.21) | copy-start | bytes 388
  28.7 8.3 %copy-start.6 = (s32[32]{0:T(128)S(1)}, s32[32]{0:T(128)}, u32[]{:S(2)}) copy-start(s32[32]{0:T(128)} %param.19) | copy-start | bytes 388
  28.7 154.3 %all-to-all-start = ((bf16[16,32,8192]{2,1,0:T(8,128)(2,1)}), bf16[16,32,8192]{2,1,0:T(8,128)(2,1)}, u32[]{:S(2)}, u32[]{:S(2)}) async-start(bf16[16,32,8192]{2,1,0:T(8,128)(2,1)} %copy.64), calls=%async_computation | async-start | bytes 16777216 | tf_op jit(solution)/shard_map/all_to_all | solution.py:141
  196.4 101.5 %all-to-all-start.1 = ((bf16[8,32,2,8192]{3,1,2,0:T(8,128)(2,1)}), bf16[8,32,2,8192]{3,1,2,0:T(8,128)(2,1)}, u32[]{:S(2)}, u32[]{:S(2)}) async-start(bf16[8,32,2,8192]{3,1,2,0:T(8,128)(2,1)} %stack.2), calls=%async_computation.1 | async-start | bytes 16777216 | tf_op jit(solution)/shard_map/all_to_all | solution.py:36
  204.0 267.5 %reduce-scatter.2.cloned.1.call-start = ((), (), s32[]{:S(2)}) async-start(), calls=%async_computation.4 | async-start | bytes 9437184 | tf_op jit(solution)/shard_map/reduce_scatter | solution.py:158
  297.8 7.7 %copy-start.3 = (bf16[8192,128]{1,0:T(8,128)(2,1)S(1)}, bf16[8192,128]{1,0:T(8,128)(2,1)}, u32[]{:S(2)}) copy-start(bf16[8192,128]{1,0:T(8,128)(2,1)} %param.14) | copy-start | bytes 6291460
  305.6 7.1 %copy-start.2 = (bf16[8,32,2,8192]{3,1,0,2:T(8,128)(2,1)S(1)}, bf16[8,32,2,8192]{3,1,0,2:T(8,128)(2,1)}, u32[]{:S(2)}) copy-start(bf16[8,32,2,8192]{3,1,0,2:T(8,128)(2,1)} %copy.67) | copy-start | bytes 25165828
  312.6 7.2 %copy-start.7 = (bf16[2,2048,128]{2,1,0:T(8,128)(2,1)S(1)}, bf16[2,2048,128]{2,1,0:T(8,128)(2,1)}, u32[]{:S(2)}) copy-start(bf16[2,2048,128]{2,1,0:T(8,128)(2,1)} %param.17) | copy-start | bytes 3145732
  411.5 62.6 %copy-start.1 = (bf16[8192,128]{1,0:T(8,128)(2,1)S(1)}, bf16[8192,128]{1,0:T(8,128)(2,1)}, u32[]{:S(2)}) copy-start(bf16[8192,128]{1,0:T(8,128)(2,1)} %param.15) | copy-start | bytes 6291460
Sparse Core Ops, SparseCore 0:
  421.9 49.6 reduce-scatter.1
